TPU v7x, 256 devices: a whole 4x4x8 slice. The times are simulated.
256 devices in a mesh: seq: 32 (over x, z_hi, core), tensor: 8 (over z_lo, y).
Axes of the slice: x: 4, y: 4, z: 8 (z_hi: 4, z_lo: 2; z = z_hi * 2 + z_lo), core: 2. Of those that a mesh axis runs over, the one named last changes fastest.
Arguments:
- keyval: bfloat16 [16384, 8192], P('seq', 'tensor'), may hold values from -6 to 6
- gating: bfloat16 [16384, 8192], P('seq', 'tensor'), may hold values from -6 to 6
- skip_gain: float32 [8192], P('tensor'), may hold values from -4 to 4
- filter_values: float32 [2, 64, 2, 32, 8192], P(None, None, None, 'seq', 'tensor'), may hold values from -12 to 12
- blocks: int32 [64, 64], P('tensor'), may hold values from 0 to 255, as said below
- out_weight: bfloat16 [8192, 8192], P('seq', 'tensor'), may hold values from -0.0625 to 0.0625
Outputs:
- mixed: bfloat16 [16384, 8192], P('seq', 'tensor')
Inputs may be any that keep to these rules, and one draw needn't show every extreme that they name: Each row names 64 different blocks.
All inputs are finite; a program needn't handle non-finite values.
Results may differ from a plain program's by a relative error of at most 0.0063.
Values may be sent and summed in bfloat16 or wider, within the bound.
A program may use at most 128 MiB of HBM per device.

v0:
```python
import math
import jax
import jax.numpy as jnp
from jax import lax
from jax.sharding import PartitionSpec as P

BLOCK = 64
HIGHEST = lax.Precision.HIGHEST


def tables(first_index, second_index, length):
    phase = first_index * second_index % length
    angle = 2.0 * math.pi / length * phase.astype(jnp.float32)
    return (jnp.cos(angle), jnp.sin(angle))


def rounded(value):
    return lax.optimization_barrier(value.astype(jnp.bfloat16)).astype(jnp.float32)


def whole_conv(signal_group, block_list, filter_group, cycle_size, tokens_local):
    seq_length = cycle_size * tokens_local
    unit = signal_group.shape[1]
    repeat = filter_group.shape[2]
    signal = signal_group.astype(jnp.float32).reshape(cycle_size, tokens_local, unit)
    cycle_index = jnp.arange(cycle_size, dtype=jnp.int32)
    local_index = jnp.arange(tokens_local, dtype=jnp.int32)
    cosine_cycle, sine_cycle = tables(cycle_index[:, None], cycle_index[None, :], cycle_size)
    first_real = jnp.einsum("pa,ajc->pjc", cosine_cycle, signal, precision=HIGHEST)
    first_imaginary = -jnp.einsum("pa,ajc->pjc", sine_cycle, signal, precision=HIGHEST)
    cosine_twist, sine_twist = tables(cycle_index[:, None], local_index[None, :], seq_length)
    cosine_twist = cosine_twist[:, :, None]
    sine_twist = sine_twist[:, :, None]
    twist_real = rounded(first_real * cosine_twist + first_imaginary * sine_twist)
    twist_imaginary = rounded(first_imaginary * cosine_twist - first_real * sine_twist)
    kept_rows = (
        block_list[:, None] * repeat + jnp.arange(repeat, dtype=jnp.int32)[None, :]
    ).reshape(-1)
    cosine_kept, sine_kept = tables(kept_rows[:, None], local_index[None, :], tokens_local)
    spectrum_real = jnp.einsum(
        "qj,pjc->pqc", cosine_kept, twist_real, precision=HIGHEST
    ) + jnp.einsum("qj,pjc->pqc", sine_kept, twist_imaginary, precision=HIGHEST)
    spectrum_imaginary = jnp.einsum(
        "qj,pjc->pqc", cosine_kept, twist_imaginary, precision=HIGHEST
    ) - jnp.einsum("qj,pjc->pqc", sine_kept, twist_real, precision=HIGHEST)
    filter_real = filter_group[0].reshape(-1, cycle_size, unit).transpose(1, 0, 2)
    filter_imaginary = filter_group[1].reshape(-1, cycle_size, unit).transpose(1, 0, 2)
    product_real = filter_real * spectrum_real - filter_imaginary * spectrum_imaginary
    product_imaginary = filter_real * spectrum_imaginary + filter_imaginary * spectrum_real
    back_real = jnp.einsum(
        "qj,pqc->pjc", cosine_kept, product_real, precision=HIGHEST
    ) - jnp.einsum("qj,pqc->pjc", sine_kept, product_imaginary, precision=HIGHEST)
    back_imaginary = jnp.einsum(
        "qj,pqc->pjc", sine_kept, product_real, precision=HIGHEST
    ) + jnp.einsum("qj,pqc->pjc", cosine_kept, product_imaginary, precision=HIGHEST)
    turned_real = rounded(back_real * cosine_twist - back_imaginary * sine_twist)
    turned_imaginary = rounded(back_real * sine_twist + back_imaginary * cosine_twist)
    convolved = (
        jnp.einsum("pa,pjc->ajc", cosine_cycle, turned_real, precision=HIGHEST)
        - jnp.einsum("pa,pjc->ajc", sine_cycle, turned_imaginary, precision=HIGHEST)
    ) / seq_length
    return convolved.astype(jnp.bfloat16).reshape(seq_length, unit)


def body(keyval, gating, skip_gain, filter_values, blocks, out_weight):
    cycle_size = lax.axis_size("seq")
    cycle_pos = lax.axis_index("seq")
    tokens_local, channels = keyval.shape
    seq_length = tokens_local * cycle_size
    repeat = BLOCK // cycle_size
    groups_local = blocks.shape[0]
    group_width = channels // groups_local
    whole_weight = lax.all_gather(out_weight, "seq", axis=0, tiled=True)
    narrow = channels // cycle_size
    unit = min(narrow, group_width)
    subgroups = narrow // unit
    columns = lax.all_to_all(keyval, "seq", split_axis=1, concat_axis=0, tiled=True)
    filter_cols = lax.all_to_all(filter_values, "seq", split_axis=4, concat_axis=3, tiled=True)
    sub_group = (cycle_pos * narrow + jnp.arange(subgroups, dtype=jnp.int32) * unit) // group_width
    match = sub_group[:, None, None] == jnp.arange(groups_local, dtype=jnp.int32)[None, :, None]
    sub_blocks = jnp.sum(jnp.where(match, blocks[None, :, :], 0), axis=1)
    sub_signal = columns.reshape(seq_length, subgroups, unit).transpose(1, 0, 2)
    sub_filters = filter_cols.reshape(
        2, filter_cols.shape[1], repeat, cycle_size, subgroups, unit
    ).transpose(4, 0, 1, 2, 3, 5)

    def sub_step(items):
        return whole_conv(items[0], items[1], items[2], cycle_size, tokens_local)

    done = lax.map(sub_step, (sub_signal, sub_blocks, sub_filters))
    done = done.transpose(1, 0, 2).reshape(seq_length, narrow)
    convolved = lax.all_to_all(done, "seq", split_axis=0, concat_axis=1, tiled=True)
    hidden = (
        gating.astype(jnp.float32)
        * (convolved.astype(jnp.float32) + skip_gain[None, :] * keyval.astype(jnp.float32))
    ).astype(jnp.bfloat16)
    full_hidden = lax.all_gather(hidden, "tensor", axis=1, tiled=True)
    mixed_rows = jnp.dot(full_hidden, whole_weight, preferred_element_type=jnp.float32)
    return mixed_rows.astype(jnp.bfloat16)


def solution(mesh):
    placed = (
        P("seq", "tensor"),
        P("seq", "tensor"),
        P("tensor"),
        P(None, None, None, "seq", "tensor"),
        P("tensor", None),
        P("seq", "tensor"),
    )
    return jax.shard_map(
        body, mesh=mesh, in_specs=placed, out_specs=P("seq", "tensor"), check_vma=False
    )
```

profile of v0, /device:TPU:33, one launch (start us, length us, event | category | flops | bytes accessed | tf_op | source)
XLA Modules:
  0.0 406.2 jit_solution(17398672774952115893)
XLA Ops:
  6.5 2.3 copy.54
  8.8 10.9 %all-to-all-start.1 = ((bf16[512,32,32]{0,2,1:T(8,128)(2,1)}), bf16[512,32,32]{0,2,1:T(8,128)(2,1)S(1)}, u32[]{:S(2)}, u32[]{:S(2)}) async-start(bf16[512,32,32]{0,2,1:T(8,128)(2,1)} %bitcast.3), calls=%async_computation.1 | async-start | bytes 2097152 | tf_op jit(solution)/shard_map/all_to_all | solution.py:77
  19.7 4.2 %copy.51 = f32[2,64,2,1,1024]{1,2,3,0,4:T(2,128)S(1)} copy(f32[2,64,2,1,1024]{4,3,2,1,0:T(1,128)} %param.9) | data formatting | bytes 2097152 | tf_op args[3]
  23.9 3.2 reshape.112
  27.2 21.8 %all-to-all-done.1 = bf16[512,32,32]{0,2,1:T(8,128)(2,1)S(1)} async-done(((bf16[512,32,32]{0,2,1:T(8,128)(2,1)}), bf16[512,32,32]{0,2,1:T(8,128)(2,1)S(1)}, u32[]{:S(2)}, u32[]{:S(2)}) %all-to-all-start.1) | async-done | bytes 1048608 | tf_op jit(solution)/shard_map/all_to_all | solution.py:77
  49.0 4.8 %all-to-all-start = ((f32[32,1,8192]{2,1,0:T(1,128)}), f32[32,1,8192]{2,1,0:T(1,128)S(1)}, u32[]{:S(2)}, u32[]{:S(2)}) async-start(f32[32,1,8192]{2,1,0:T(1,128)} %reshape.112), calls=%async_computation | async-start | bytes 2097152 | tf_op jit(solution)/shard_map/all_to_all | solution.py:78
  54.3 1.5 fusion.6
  55.8 2.0 add_convert_fusion.1
  57.9 2.5 fusion.13
  60.3 3.3 fusion.17
  63.6 3.3 fusion.2
  66.9 16.2 %all-to-all-done = f32[32,1,8192]{2,1,0:T(1,128)S(1)} async-done(((f32[32,1,8192]{2,1,0:T(1,128)}), f32[32,1,8192]{2,1,0:T(1,128)S(1)}, u32[]{:S(2)}, u32[]{:S(2)}) %all-to-all-start) | async-done | bytes 1048608 | tf_op jit(solution)/shard_map/all_to_all | solution.py:78
  83.6 16.2 %reduce.2 = f32[32,8192]{1,0:T(8,128)S(1)} reduce(f32[32,1,8192]{2,1,0:T(1,128)S(1)} %all-to-all-done, f32[]{:T(128)} %broadcast.243), dimensions={1}, to_apply=%all_to_all.12.reduce_sub_computation | reduce | bytes 2097156 | tf_op jit(solution)/shard_map/all_to_all | solution.py:78
  101.3 1.7 fusion.121
  103.0 2.1 copy.52
  105.2 1.9 squeeze.17
  107.1 2.1 copy.53
  110.4 2.0 squeeze.18
  112.4 2.1 copy.61
  114.5 4.0 fusion.22
  118.5 2.8 fusion.26
  121.3 2.8 fusion.32
  124.1 2.8 convolution_add_fusion
  126.9 3.7 fusion.5
  132.1 1.6 multiply_convert_fusion
  133.8 1.6 copy.66
  135.3 4.1 %all-to-all-start.2 = ((bf16[32,512,32]{1,2,0:T(8,128)(2,1)}), bf16[32,512,32]{1,2,0:T(8,128)(2,1)S(1)}, u32[]{:S(2)}, u32[]{:S(2)}) async-start(bf16[32,512,32]{1,2,0:T(8,128)(2,1)} %copy.66), calls=%async_computation.2 | async-start | bytes 2097152 | tf_op jit(solution)/shard_map/all_to_all | solution.py:92
  140.1 29.2 %all-to-all-done.2 = bf16[32,512,32]{1,2,0:T(8,128)(2,1)S(1)} async-done(((bf16[32,512,32]{1,2,0:T(8,128)(2,1)}), bf16[32,512,32]{1,2,0:T(8,128)(2,1)S(1)}, u32[]{:S(2)}, u32[]{:S(2)}) %all-to-all-start.2) | async-done | bytes 1048608 | tf_op jit(solution)/shard_map/all_to_all | solution.py:92
  169.3 2.7 fusion.1
  172.8 88.6 %all-gather.3.cloned.1.call-done = bf16[512,8192]{0,1:T(8,128)(2,1)} async-done(((bf16[512,1024]{0,1:T(8,128)(2,1)}), bf16[512,8192]{0,1:T(8,128)(2,1)}) %all-gather.3.cloned.1.call-update) | async-done | bytes 8388624 | tf_op jit(solution)/shard_map/all_gather | solution.py:97
  261.4 122.2 %all-gather.5.cloned.1.call-done = bf16[8192,1024]{1,0:T(8,128)(2,1)} async-done(((bf16[256,1024]{1,0:T(8,128)(2,1)}), bf16[8192,1024]{1,0:T(8,128)(2,1)}) %all-gather.5.cloned.1.call-update) | async-done | bytes 16777232 | tf_op jit(solution)/shard_map/all_gather | solution.py:73
  383.5 15.6 %convolution_convert_fusion = bf16[512,1024]{1,0:T(8,128)(2,1)} fusion(bf16[512,8192]{0,1:T(8,128)(2,1)} %all-gather.3.cloned.1.call-done, bf16[8192,1024]{1,0:T(8,128)(2,1)} %all-gather.5.cloned.1.call-done), kind=kOutput, calls=%fused_computation.10 | convolution fusion | flops 8590458880 | bytes 26214400 | tf_op jit(solution)/shard_map/dot_general | solution.py:98
  (25 shorter events, 6.7 us)
Async XLA Ops:
  8.8 40.2 %all-to-all-start.1 = ((bf16[512,32,32]{0,2,1:T(8,128)(2,1)}), bf16[512,32,32]{0,2,1:T(8,128)(2,1)S(1)}, u32[]{:S(2)}, u32[]{:S(2)}) async-start(bf16[512,32,32]{0,2,1:T(8,128)(2,1)} %bitcast.3), calls=%async_computation.1 | async-start | bytes 2097152 | tf_op jit(solution)/shard_map/all_to_all | solution.py:77
  23.9 3.2 copy-start.4
  49.0 34.1 %all-to-all-start = ((f32[32,1,8192]{2,1,0:T(1,128)}), f32[32,1,8192]{2,1,0:T(1,128)S(1)}, u32[]{:S(2)}, u32[]{:S(2)}) async-start(f32[32,1,8192]{2,1,0:T(1,128)} %reshape.112), calls=%async_computation | async-start | bytes 2097152 | tf_op jit(solution)/shard_map/all_to_all | solution.py:78
  57.8 5.8 %copy-start = (bf16[32,512,32]{1,0,2:T(8,128)(2,1)}, bf16[32,512,32]{1,0,2:T(8,128)(2,1)S(1)}, u32[]{:S(2)}) copy-start(bf16[32,512,32]{1,0,2:T(8,128)(2,1)S(1)} %get-tuple-element.22) | copy-start | bytes 3145732
  110.4 4.1 %copy-start.1 = (bf16[32,512,32]{1,0,2:T(8,128)(2,1)S(1)}, bf16[32,512,32]{1,0,2:T(8,128)(2,1)}, u32[]{:S(2)}) copy-start(bf16[32,512,32]{1,0,2:T(8,128)(2,1)} %copy-done) | copy-start | bytes 3145732
  133.8 5.8 %copy-start.2 = (bf16[512,1024]{1,0:T(8,128)(2,1)S(1)}, bf16[512,1024]{1,0:T(8,128)(2,1)}, u32[]{:S(2)}) copy-start(bf16[512,1024]{1,0:T(8,128)(2,1)} %param.7) | copy-start | bytes 3145732
  135.3 34.0 %copy-start.3 = (f32[1024]{0:T(1024)S(1)}, f32[1024]{0:T(1024)}, u32[]{:S(2)}) copy-start(f32[1024]{0:T(1024)} %param.8) | copy-start | bytes 12292
  135.3 34.0 %all-to-all-start.2 = ((bf16[32,512,32]{1,2,0:T(8,128)(2,1)}), bf16[32,512,32]{1,2,0:T(8,128)(2,1)S(1)}, u32[]{:S(2)}, u32[]{:S(2)}) async-start(bf16[32,512,32]{1,2,0:T(8,128)(2,1)} %copy.66), calls=%async_computation.2 | async-start | bytes 2097152 | tf_op jit(solution)/shard_map/all_to_all | solution.py:92
  139.5 121.9 %all-gather.3.cloned.1.call-start = ((), (), s32[]{:S(2)}) async-start(), calls=%async_computation.3 | async-start | bytes 9437184 | tf_op jit(solution)/shard_map/all_gather | solution.py:97
  172.0 211.5 %all-gather.5.cloned.1.call-start = ((), (), s32[]{:S(2)}) async-start(), calls=%async_computation.4 | async-start | bytes 17301504 | tf_op jit(solution)/shard_map/all_gather | solution.py:73
Sparse Core Ops, SparseCore 0:
  172.2 89.1 all-gather.2
  263.9 119.5 all-gather.4
where the time goes:
time: 410 us; the launch traced here: 406 us
  waiting for transfers between devices  279 us (68%)
  matrix products  47.4 us (12%)
  local copies, waits for them, and re-layouts  27.1 us (7%)
  starting transfers between devices  19.8 us (5%)
  other arithmetic  19.3 us (5%)
  between operations  13.8 us (3%)
    all_gather x1, waiting for transfers between devices, body(): whole_weight = lax.all_gather(out_weight, 'seq', axis=0, tiled=True)  122 us
    all_gather x1, waiting for transfers between devices, body(): full_hidden = lax.all_gather(hidden, 'tensor', axis=1, tiled=True)  88.6 us
    all_to_all x1, waiting for transfers between devices, body(): lax.all_to_all(done, 'seq', split_axis=0, concat_axis=1, tiled=True)  29.2 us
    all_to_all x1, waiting for transfers between devices, body(): lax.all_to_all(keyval, 'seq', split_axis=1, concat_axis=0, tiled=True)  21.8 us
    all_to_all x1, other arithmetic, body(): lax.all_to_all(filter_values, 'seq', split_axis=4, concat_axis=3, tiled=T...  16.2 us
    all_to_all x1, waiting for transfers between devices, body(): lax.all_to_all(filter_values, 'seq', split_axis=4, concat_axis=3, tiled=T...  16.2 us
    dot_general x1, matrix products, body(): jnp.dot(full_hidden, whole_weight, preferred_element_type=jnp.float32)  15.6 us
    unnamed x15, local copies, waits for them, and re-layouts  11.7 us
  transfers between devices with their start and end apart: 5, of which 5 were waited for; matrix products, arithmetic and copies ran while one was open for 5% of the time, Pallas kernels for 0%

commit v1 on v0

--- a/solution.py
+++ b/solution.py
@@ -6,6 +6,14 @@
 
 BLOCK = 64
 HIGHEST = lax.Precision.HIGHEST
+
+
+def render_groups(values):
+    local_next = jnp.concatenate(
+        lax.all_to_all(jnp.stack(jnp.split(values, lax.axis_size("seq"), axis=0)), "seq", 0, 0),
+        axis=1,
+    )
+    return local_next
 
 
 def tables(first_index, second_index, length):
@@ -89,7 +97,7 @@
 
     done = lax.map(sub_step, (sub_signal, sub_blocks, sub_filters))
     done = done.transpose(1, 0, 2).reshape(seq_length, narrow)
-    convolved = lax.all_to_all(done, "seq", split_axis=0, concat_axis=1, tiled=True)
+    convolved = render_groups(done)
     hidden = (
         gating.astype(jnp.float32)
         * (convolved.astype(jnp.float32) + skip_gain[None, :] * keyval.astype(jnp.float32))

time: 410 us -> 410 us (level)
  no operation moved by 1% of the time
where the time goes in v1:
time: 410 us; the launch traced here: 406 us
  waiting for transfers between devices  279 us (68%)
  matrix products  47.4 us (12%)
  local copies, waits for them, and re-layouts  27.1 us (7%)
  starting transfers between devices  19.8 us (5%)
  other arithmetic  19.3 us (5%)
  between operations  13.8 us (3%)
    all_gather x1, waiting for transfers between devices, body(): whole_weight = lax.all_gather(out_weight, 'seq', axis=0, tiled=True)  122 us
    all_gather x1, waiting for transfers between devices, body(): full_hidden = lax.all_gather(hidden, 'tensor', axis=1, tiled=True)  88.6 us
    all_to_all x1, waiting for transfers between devices, render_groups(): lax.all_to_all(jnp.stack(jnp.split(values, lax.axis_size('seq'), axis=0))...  29.2 us
    all_to_all x1, waiting for transfers between devices, body(): lax.all_to_all(keyval, 'seq', split_axis=1, concat_axis=0, tiled=True)  21.8 us
    all_to_all x1, other arithmetic, body(): lax.all_to_all(filter_values, 'seq', split_axis=4, concat_axis=3, tiled=T...  16.2 us
    all_to_all x1, waiting for transfers between devices, body(): lax.all_to_all(filter_values, 'seq', split_axis=4, concat_axis=3, tiled=T...  16.2 us
    dot_general x1, matrix products, body(): jnp.dot(full_hidden, whole_weight, preferred_element_type=jnp.float32)  15.6 us
    unnamed x15, local copies, waits for them, and re-layouts  11.7 us
  transfers between devices with their start and end apart: 5, of which 5 were waited for; matrix products, arithmetic and copies ran while one was open for 5% of the time, Pallas kernels for 0%

profile of v1, /device:TPU:33, one launch (start us, length us, event | category | flops | bytes accessed | tf_op | source)
XLA Modules:
  0.0 406.2 jit_solution(17398672774952115893)
XLA Ops:
  6.5 2.3 copy.54
  8.8 10.9 %all-to-all-start.1 = ((bf16[512,32,32]{0,2,1:T(8,128)(2,1)}), bf16[512,32,32]{0,2,1:T(8,128)(2,1)S(1)}, u32[]{:S(2)}, u32[]{:S(2)}) async-start(bf16[512,32,32]{0,2,1:T(8,128)(2,1)} %bitcast.3), calls=%async_computation.1 | async-start | bytes 2097152 | tf_op jit(solution)/shard_map/all_to_all | solution.py:85
  19.7 4.2 %copy.51 = f32[2,64,2,1,1024]{1,2,3,0,4:T(2,128)S(1)} copy(f32[2,64,2,1,1024]{4,3,2,1,0:T(1,128)} %param.9) | data formatting | bytes 2097152 | tf_op args[3]
  23.9 3.2 reshape.174
  27.2 21.8 %all-to-all-done.1 = bf16[512,32,32]{0,2,1:T(8,128)(2,1)S(1)} async-done(((bf16[512,32,32]{0,2,1:T(8,128)(2,1)}), bf16[512,32,32]{0,2,1:T(8,128)(2,1)S(1)}, u32[]{:S(2)}, u32[]{:S(2)}) %all-to-all-start.1) | async-done | bytes 1048608 | tf_op jit(solution)/shard_map/all_to_all | solution.py:85
  49.0 4.8 %all-to-all-start = ((f32[32,1,8192]{2,1,0:T(1,128)}), f32[32,1,8192]{2,1,0:T(1,128)S(1)}, u32[]{:S(2)}, u32[]{:S(2)}) async-start(f32[32,1,8192]{2,1,0:T(1,128)} %reshape.174), calls=%async_computation | async-start | bytes 2097152 | tf_op jit(solution)/shard_map/all_to_all | solution.py:86
  54.3 1.5 fusion.6
  55.8 2.0 add_convert_fusion.1
  57.9 2.5 fusion.13
  60.3 3.3 fusion.17
  63.6 3.3 fusion.2
  66.9 16.2 %all-to-all-done = f32[32,1,8192]{2,1,0:T(1,128)S(1)} async-done(((f32[32,1,8192]{2,1,0:T(1,128)}), f32[32,1,8192]{2,1,0:T(1,128)S(1)}, u32[]{:S(2)}, u32[]{:S(2)}) %all-to-all-start) | async-done | bytes 1048608 | tf_op jit(solution)/shard_map/all_to_all | solution.py:86
  83.6 16.2 %reduce.2 = f32[32,8192]{1,0:T(8,128)S(1)} reduce(f32[32,1,8192]{2,1,0:T(1,128)S(1)} %all-to-all-done, f32[]{:T(128)} %broadcast.243), dimensions={1}, to_apply=%all_to_all.22.reduce_sub_computation | reduce | bytes 2097156 | tf_op jit(solution)/shard_map/all_to_all | solution.py:86
  101.3 1.7 fusion.121
  103.0 2.1 copy.52
  105.2 1.9 squeeze.17
  107.1 2.1 copy.53
  110.4 2.0 squeeze.18
  112.4 2.1 copy.61
  114.5 4.0 fusion.22
  118.5 2.8 fusion.26
  121.3 2.8 fusion.32
  124.1 2.8 convolution_add_fusion
  126.9 3.7 fusion.5
  132.1 1.6 multiply_convert_fusion
  133.8 1.6 copy.66
  135.3 4.1 %all-to-all-start.2 = ((bf16[32,512,32]{1,2,0:T(8,128)(2,1)}), bf16[32,512,32]{1,2,0:T(8,128)(2,1)S(1)}, u32[]{:S(2)}, u32[]{:S(2)}) async-start(bf16[32,512,32]{1,2,0:T(8,128)(2,1)} %copy.66), calls=%async_computation.2 | async-start | bytes 2097152 | tf_op jit(solution)/shard_map/all_to_all | solution.py:13
  140.1 29.2 %all-to-all-done.2 = bf16[32,512,32]{1,2,0:T(8,128)(2,1)S(1)} async-done(((bf16[32,512,32]{1,2,0:T(8,128)(2,1)}), bf16[32,512,32]{1,2,0:T(8,128)(2,1)S(1)}, u32[]{:S(2)}, u32[]{:S(2)}) %all-to-all-start.2) | async-done | bytes 1048608 | tf_op jit(solution)/shard_map/all_to_all | solution.py:13
  169.3 2.7 fusion.1
  172.8 88.6 %all-gather.3.cloned.1.call-done = bf16[512,8192]{0,1:T(8,128)(2,1)} async-done(((bf16[512,1024]{0,1:T(8,128)(2,1)}), bf16[512,8192]{0,1:T(8,128)(2,1)}) %all-gather.3.cloned.1.call-update) | async-done | bytes 8388624 | tf_op jit(solution)/shard_map/all_gather | solution.py:105
  261.4 122.2 %all-gather.5.cloned.1.call-done = bf16[8192,1024]{1,0:T(8,128)(2,1)} async-done(((bf16[256,1024]{1,0:T(8,128)(2,1)}), bf16[8192,1024]{1,0:T(8,128)(2,1)}) %all-gather.5.cloned.1.call-update) | async-done | bytes 16777232 | tf_op jit(solution)/shard_map/all_gather | solution.py:81
  383.5 15.6 %convolution_convert_fusion = bf16[512,1024]{1,0:T(8,128)(2,1)} fusion(bf16[512,8192]{0,1:T(8,128)(2,1)} %all-gather.3.cloned.1.call-done, bf16[8192,1024]{1,0:T(8,128)(2,1)} %all-gather.5.cloned.1.call-done), kind=kOutput, calls=%fused_computation.10 | convolution fusion | flops 8590458880 | bytes 26214400 | tf_op jit(solution)/shard_map/dot_general | solution.py:106
  (25 shorter events, 6.7 us)
Async XLA Ops:
  8.8 40.2 %all-to-all-start.1 = ((bf16[512,32,32]{0,2,1:T(8,128)(2,1)}), bf16[512,32,32]{0,2,1:T(8,128)(2,1)S(1)}, u32[]{:S(2)}, u32[]{:S(2)}) async-start(bf16[512,32,32]{0,2,1:T(8,128)(2,1)} %bitcast.3), calls=%async_computation.1 | async-start | bytes 2097152 | tf_op jit(solution)/shard_map/all_to_all | solution.py:85
  23.9 3.2 copy-start.4
  49.0 34.1 %all-to-all-start = ((f32[32,1,8192]{2,1,0:T(1,128)}), f32[32,1,8192]{2,1,0:T(1,128)S(1)}, u32[]{:S(2)}, u32[]{:S(2)}) async-start(f32[32,1,8192]{2,1,0:T(1,128)} %reshape.174), calls=%async_computation | async-start | bytes 2097152 | tf_op jit(solution)/shard_map/all_to_all | solution.py:86
  57.8 5.8 %copy-start = (bf16[32,512,32]{1,0,2:T(8,128)(2,1)}, bf16[32,512,32]{1,0,2:T(8,128)(2,1)S(1)}, u32[]{:S(2)}) copy-start(bf16[32,512,32]{1,0,2:T(8,128)(2,1)S(1)} %get-tuple-element.22) | copy-start | bytes 3145732
  110.4 4.1 %copy-start.1 = (bf16[32,512,32]{1,0,2:T(8,128)(2,1)S(1)}, bf16[32,512,32]{1,0,2:T(8,128)(2,1)}, u32[]{:S(2)}) copy-start(bf16[32,512,32]{1,0,2:T(8,128)(2,1)} %copy-done) | copy-start | bytes 3145732
  133.8 5.8 %copy-start.2 = (bf16[512,1024]{1,0:T(8,128)(2,1)S(1)}, bf16[512,1024]{1,0:T(8,128)(2,1)}, u32[]{:S(2)}) copy-start(bf16[512,1024]{1,0:T(8,128)(2,1)} %param.7) | copy-start | bytes 3145732
  135.3 34.0 %copy-start.3 = (f32[1024]{0:T(1024)S(1)}, f32[1024]{0:T(1024)}, u32[]{:S(2)}) copy-start(f32[1024]{0:T(1024)} %param.8) | copy-start | bytes 12292
  135.3 34.0 %all-to-all-start.2 = ((bf16[32,512,32]{1,2,0:T(8,128)(2,1)}), bf16[32,512,32]{1,2,0:T(8,128)(2,1)S(1)}, u32[]{:S(2)}, u32[]{:S(2)}) async-start(bf16[32,512,32]{1,2,0:T(8,128)(2,1)} %copy.66), calls=%async_computation.2 | async-start | bytes 2097152 | tf_op jit(solution)/shard_map/all_to_all | solution.py:13
  139.5 121.9 %all-gather.3.cloned.1.call-start = ((), (), s32[]{:S(2)}) async-start(), calls=%async_computation.3 | async-start | bytes 9437184 | tf_op jit(solution)/shard_map/all_gather | solution.py:105
  172.0 211.5 %all-gather.5.cloned.1.call-start = ((), (), s32[]{:S(2)}) async-start(), calls=%async_computation.4 | async-start | bytes 17301504 | tf_op jit(solution)/shard_map/all_gather | solution.py:81
Sparse Core Ops, SparseCore 0:
  172.2 89.1 all-gather.2
  263.9 119.5 all-gather.4
